TPU v7x, 32 devices: a whole 2x2x4 slice. The times are simulated.
32 devices in a mesh: seq: 16 (over z, x, core), head: 2 (over y).
Axes of the slice: x: 2, y: 2, z: 4, core: 2. Of those that a mesh axis runs over, the one named last changes fastest.
Arguments:
- queries: bfloat16 [16384, 128], P('seq'), may hold values from -0.59765625 to 0.59765625
- key_rows: bfloat16 [16384, 128], P('seq'), may hold values from -0.59765625 to 0.59765625
- value_rows: bfloat16 [16384, 4096], P('seq', 'head'), may hold values from -0.119628906 to 0.119628906
- out_grad: bfloat16 [16384, 4096], P('seq', 'head'), may hold values from -0.29882812 to 0.29882812
- level_index: int32 [16384, 5], P('seq'), may hold values from 0 to 7
- level_table: float32 [5, 8, 64], P(None, None, 'head'), may hold values from 0.25 to 2.5
Outputs:
- query_grad: bfloat16 [16384, 128], P('seq')
- key_grad: bfloat16 [16384, 128], P('seq')
- value_grad: bfloat16 [16384, 4096], P('seq', 'head')
All inputs are finite; a program needn't handle non-finite values.
Results may differ from a plain program's by a relative error of at most 0.018.
Values may be sent and summed in bfloat16 or wider, within the bound.
No kernel may reach another device: no remote copies, remote signals or barrier semaphores. Data moves between devices by JAX's collectives and lax.ppermute only.
A program may use at most 128 MiB of HBM per device.

v0:
```python
import jax
import jax.numpy as jnp
from jax import lax
from jax.sharding import PartitionSpec as P


def swapped(block, axis, stride):
    count = lax.axis_size(axis)
    route = []
    for low in range(count):
        high = low | 1 << stride
        if high != low and high < count:
            route += [(low, high), (high, low)]
    return lax.ppermute(block, axis, route)


def contract_rows(left, right):
    return lax.dot_general(
        left, right, (((0,), (0,)), ((), ())), preferred_element_type=jnp.float32
    )


def contract_cols(left, right):
    return lax.dot_general(
        left, right, (((1,), (1,)), ((), ())), preferred_element_type=jnp.float32
    )


def per_device(queries, key_rows, value_rows, out_grad, level_index, level_table):
    rows_here = queries.shape[0]
    columns = value_rows.shape[1]
    heads_here = level_table.shape[2]
    head_size = columns // heads_here
    table_rows = level_table.shape[1]
    tree_depth = lax.axis_size("seq").bit_length() - 1
    position = lax.axis_index("seq")
    matches = level_index[:, :, None] == jnp.arange(table_rows, dtype=jnp.int32)[None, None, :]
    weights = jnp.sum(jnp.where(matches[:, :, :, None], level_table[None], 0.0), axis=2)
    shaped = out_grad.astype(jnp.float32).reshape(rows_here, heads_here, head_size)

    def scale_by(height):
        return (
            (shaped * weights[:, height, :, None]).reshape(rows_here, columns).astype(jnp.bfloat16)
        )

    local_scaled = scale_by(0)
    scaled_list = [scale_by(height + 1) for height in range(tree_depth)]
    flags = [position >> height & 1 == 1 for height in range(tree_depth)]
    level_grads = []
    for height in range(tree_depth):
        product = contract_rows(queries, scaled_list[height])
        level_grads.append(jnp.where(flags[height], product, jnp.zeros_like(product)))
    block_state = contract_rows(key_rows, value_rows).astype(jnp.bfloat16)
    siblings = []
    block_sum = block_state
    for height in range(tree_depth):
        partner = swapped(block_sum, "seq", height)
        siblings.append(jnp.where(flags[height], partner, jnp.zeros_like(partner)))
        block_sum = (block_sum.astype(jnp.float32) + partner.astype(jnp.float32)).astype(
            jnp.bfloat16
        )
    pending = jnp.stack(level_grads)
    state_grad = jnp.zeros(block_state.shape, jnp.float32)
    for height in range(tree_depth):
        arrived = swapped(pending.astype(jnp.bfloat16), "seq", height).astype(pending.dtype)
        state_grad = state_grad + jnp.where(flags[height], jnp.zeros_like(arrived[0]), arrived[0])
        pending = pending[1:] + arrived[1:]
    row_ids = lax.broadcasted_iota(jnp.int32, (rows_here, rows_here), 0)
    col_ids = lax.broadcasted_iota(jnp.int32, (rows_here, rows_here), 1)
    causal = row_ids >= col_ids
    scores = contract_cols(queries, key_rows)
    masked = jnp.where(causal, scores, 0.0).astype(jnp.bfloat16)
    score_grad = jnp.where(causal, contract_cols(local_scaled, value_rows), 0.0).astype(
        jnp.bfloat16
    )
    state_low = state_grad.astype(jnp.bfloat16)
    value_grad = contract_rows(masked, local_scaled) + jnp.dot(
        key_rows, state_low, preferred_element_type=jnp.float32
    )
    query_grad = jnp.dot(score_grad, key_rows, preferred_element_type=jnp.float32)
    for height in range(tree_depth):
        query_grad = query_grad + contract_cols(scaled_list[height], siblings[height])
    key_grad = contract_rows(score_grad, queries) + contract_cols(value_rows, state_low)
    query_grad, key_grad = (
        lax.psum(query_grad.astype(jnp.bfloat16), "head").astype(jnp.float32),
        lax.psum(key_grad.astype(jnp.bfloat16), "head").astype(jnp.float32),
    )
    return (
        query_grad.astype(jnp.bfloat16),
        key_grad.astype(jnp.bfloat16),
        value_grad.astype(jnp.bfloat16),
    )


def solution(mesh):
    return jax.shard_map(
        per_device,
        mesh=mesh,
        in_specs=(
            P("seq", None),
            P("seq", None),
            P("seq", "head"),
            P("seq", "head"),
            P("seq", None),
            P(None, None, "head"),
        ),
        out_specs=(P("seq", None), P("seq", None), P("seq", "head")),
        check_vma=False,
    )
```

profile of v0, /device:TPU:15, one launch (start us, length us, event | category | flops | bytes accessed | tf_op | source)
XLA Modules:
  0.0 204.7 jit_solution(11450597541478447088)
XLA Ops:
  7.2 0.0 copy-start
  7.2 0.0 all-reduce.3.cloned.1.call-start
  7.2 0.8 iota_compare_fusion.1
  8.1 1.7 select_reduce_fusion
  9.8 0.1 slice_bitcast_fusion.2
  9.8 6.4 %copy.16 = bf16[1024,2048]{0,1:T(8,128)(2,1)} copy(bf16[1024,2048]{1,0:T(8,128)(2,1)} %param.9) | data formatting | bytes 8388608 | tf_op args[3]
  16.2 8.7 %fusion.2 = (bf16[1024,2048]{0,1:T(8,128)(2,1)S(1)}, bf16[1024,2048]{0,1:T(8,128)(2,1)S(1)}, bf16[1024,2048]{0,1:T(8,128)(2,1)S(1)}, bf16[1024,2048]{0,1:T(8,128)(2,1)S(1)}, bf16[1024,2048]{0,1:T(8,128)(2,1)}) fusion(bf16[1024,2048]{0,1:T(8,128)(2,1)} %copy.16, f32[1024,32]{0,1:T(8,128)S(1)} %get-tuple-element.14, f32[1024,32]{0,1:T(8,128)S(1)} %get-tuple-element.17, ...), kind=kLoop, calls=%fused_computation.7 | loop fusion | flops 23068672 | bytes 25821184 | tf_op jit(solution)/shard_map/convert_element_type | solution.py:43
  24.9 1.3 fusion.46
  26.2 1.3 fusion.45
  27.5 0.7 copy-done.5
  28.1 1.3 fusion.10
  29.4 0.0 copy-start.7
  29.4 1.3 fusion.47
  30.7 0.0 copy-start.14
  30.7 0.3 pad_maximum_fusion
  31.0 0.7 collective-permute-start.4
  31.7 0.6 copy-done.7
  32.3 1.5 convolution_convert_fusion
  33.9 0.7 collective-permute-start
  34.6 4.8 %select_convert_fusion.1 = bf16[1024,1024]{1,0:T(8,128)(2,1)S(1)} fusion(bf16[1024,2048]{0,1:T(8,128)(2,1)S(1)} %copy-done.14, bf16[1024,2048]{1,0:T(8,128)(2,1)S(1)} %copy-done.7), kind=kOutput, calls=%fused_computation.14 | convolution fusion | flops 4298113024 | bytes 10485760 | tf_op jit(solution)/shard_map/dot_general | solution.py:24
  39.3 0.0 collective-permute-done.4
  39.4 0.3 convert_element_type.108
  39.6 2.8 %fusion.44 = (bf16[3,128,2048]{1,2,0:T(8,128)(2,1)}, f32[3,128,2048]{1,2,0:T(8,128)}) fusion(f32[4,128,2048]{1,2,0:T(8,128)S(1)} %convert_element_type.108, f32[1,128,2048]{1,2,0:T(8,128)S(1)} %get-tuple-element.20, f32[1,128,2048]{1,2,0:T(8,128)S(1)} %get-tuple-element.22, f32[1,128,2048]{1,2,0:T(8,128)S(1)} %get-tuple-element.24), kind=kLoop, calls=%fused_computation.78 | loop fusion | flops 3145728 | bytes 11010048 | tf_op jit(solution)/shard_map/convert_element_type | solution.py:65
  42.4 0.6 copy-done.11
  43.1 0.3 collective-permute-start.5
  43.3 9.3 %fusion.11 = f32[1024,2048]{1,0:T(8,128)} fusion(bf16[1024,2048]{0,1:T(8,128)(2,1)} %get-tuple-element.13, bf16[1024,128]{1,0:T(8,128)(2,1)S(1)} %copy-done.13, bf16[1024,128]{1,0:T(8,128)(2,1)S(1)} %copy-done), kind=kOutput, calls=%fused_computation.29 | convolution fusion | flops 4566548480 | bytes 13107200 | tf_op jit(solution)/shard_map/dot_general | solution.py:18
  52.7 0.0 collective-permute-done
  52.7 1.2 add_convert_fusion.2
  53.8 1.3 collective-permute-start.1
  55.1 0.7 fusion.49
  55.9 0.7 fusion.48
  56.6 33.9 %collective-permute-done.1 = bf16[128,2048]{1,0:T(8,128)(2,1)S(1)} collective-permute-done((bf16[128,2048]{1,0:T(8,128)(2,1)S(1)}, bf16[128,2048]{1,0:T(8,128)(2,1)S(1)}, u32[]{:S(2)}, u32[]{:S(2)}) %collective-permute-start.1) | collective-permute-done | bytes 524320 | tf_op jit(solution)/shard_map/ppermute | solution.py:14
  90.5 0.1 add_convert_fusion.1
  90.6 0.2 collective-permute-start.2
  90.8 0.0 collective-permute-done.5
  90.8 1.6 convert_element_type.110
  92.5 0.3 fusion.43
  92.8 1.4 collective-permute-start.6
  94.1 0.5 copy-done.10
  94.6 1.3 convolution_add_fusion.1
  96.0 7.3 %collective-permute-done.2 = bf16[128,2048]{1,0:T(8,128)(2,1)S(1)} collective-permute-done((bf16[128,2048]{1,0:T(8,128)(2,1)S(1)}, bf16[128,2048]{1,0:T(8,128)(2,1)S(1)}, u32[]{:S(2)}, u32[]{:S(2)}) %collective-permute-start.2) | collective-permute-done | bytes 524320 | tf_op jit(solution)/shard_map/ppermute | solution.py:14
  103.3 0.1 add_convert_fusion
  103.4 2.4 %collective-permute-start.3 = (bf16[128,2048]{1,0:T(8,128)(2,1)S(1)}, bf16[128,2048]{1,0:T(8,128)(2,1)S(1)}, u32[]{:S(2)}, u32[]{:S(2)}) collective-permute-start(bf16[128,2048]{1,0:T(8,128)(2,1)S(1)} %add_convert_fusion), channel_id=1, source_target_pairs={{0,16},{16,0},{2,18},{18,2},{4,20},{20,4},{6,22},{22,6},{8,24},{24... | collective-permute-start | bytes 1572872 | tf_op jit(solution)/shard_map/ppermute | solution.py:14
  105.8 0.0 copy-done.6
  105.8 1.3 fusion.26
  107.1 27.9 %collective-permute-done.6 = bf16[2,128,2048]{1,2,0:T(8,128)(2,1)S(1)} collective-permute-done((bf16[2,128,2048]{1,2,0:T(8,128)(2,1)S(1)}, bf16[2,128,2048]{1,2,0:T(8,128)(2,1)S(1)}, u32[]{:S(2)}, u32[]{:S(2)}) %collective-permute-start.6) | collective-permute-done | bytes 1048608 | tf_op jit(solution)/shard_map/ppermute | solution.py:14
  135.0 0.1 convert_element_type.112
  135.1 0.1 fusion.17
  135.3 4.4 %collective-permute-start.7 = (bf16[1,128,2048]{1,2,0:T(8,128)(2,1)S(1)}, bf16[1,128,2048]{1,2,0:T(8,128)(2,1)S(1)}, u32[]{:S(2)}, u32[]{:S(2)}) collective-permute-start(bf16[1,128,2048]{1,2,0:T(8,128)(2,1)S(1)} %fusion.17), channel_id=1, source_target_pairs={{0,16},{16,0},{2,18},{18,2},{4,20},{20,4},{6,22},{22,6},{8,24},{24... | collective-permute-start | bytes 1572872 | tf_op jit(solution)/shard_map/ppermute | solution.py:14
  139.7 0.0 collective-permute-done.3
  139.7 0.0 copy-done.4
  139.7 1.3 fusion.24
  141.0 0.0 copy-done.2
  141.0 0.0 copy-start.8
  141.0 2.0 fusion.15
  143.0 18.5 %collective-permute-done.7 = bf16[1,128,2048]{1,2,0:T(8,128)(2,1)S(1)} collective-permute-done((bf16[1,128,2048]{1,2,0:T(8,128)(2,1)S(1)}, bf16[1,128,2048]{1,2,0:T(8,128)(2,1)S(1)}, u32[]{:S(2)}, u32[]{:S(2)}) %collective-permute-start.7) | collective-permute-done | bytes 524320 | tf_op jit(solution)/shard_map/ppermute | solution.py:14
  161.5 1.6 fusion.20
  163.1 0.0 copy-done.8
  163.1 2.0 fusion.16
  165.1 0.0 all-reduce.3.cloned.1.call-update
  165.1 6.7 %fusion.5 = bf16[1024,2048]{1,0:T(8,128)(2,1)} fusion(f32[1024,2048]{1,0:T(8,128)} %fusion.11, bf16[1024,128]{1,0:T(8,128)(2,1)S(1)} %copy-done, bf16[1,128,2048]{1,2,0:T(8,128)(2,1)S(1)} %fusion.20), kind=kOutput, calls=%fused_computation.11 | convolution fusion | flops 541065216 | bytes 13369344 | tf_op jit(solution)/shard_map/dot_general | solution.py:77
  171.8 22.8 %all-reduce.3.cloned.1.call-done = (bf16[1024,128]{1,0:T(8,128)(2,1)}, bf16[1024,128]{1,0:T(8,128)(2,1)}) async-done(((bf16[1024,128]{1,0:T(8,128)(2,1)}, bf16[1024,128]{1,0:T(8,128)(2,1)}), (bf16[1024,128]{1,0:T(8,128)(2,1)}, bf16[1024,128]{1,0:T(8,128)(2,1)})) %all-reduce.3.cloned.1.call-update) | async-done | bytes 524304 | tf_op jit(solution)/shard_map/psum | solution.py:85
  194.5 1.7 copy.23
  196.2 1.7 copy.24
  (18 shorter events, 0.0 us)
Async XLA Ops:
  7.2 24.5 %copy-start = (bf16[1024,128]{1,0:T(8,128)(2,1)S(1)}, bf16[1024,128]{1,0:T(8,128)(2,1)}, u32[]{:S(2)}) copy-start(bf16[1024,128]{1,0:T(8,128)(2,1)} %param.7) | copy-start | bytes 786436
  7.2 187.3 %all-reduce.3.cloned.1.call-start = ((), (), s32[]{:S(2)}) async-start(), calls=%async_computation | async-start | bytes 1048576 | tf_op jit(solution)/shard_map/psum | solution.py:85
  16.2 8.7 %copy-start.13 = (bf16[1024,128]{1,0:T(8,128)(2,1)S(1)}, bf16[1024,128]{1,0:T(8,128)(2,1)}, u32[]{:S(2)}) copy-start(bf16[1024,128]{1,0:T(8,128)(2,1)} %param.6) | copy-start | bytes 786436
  24.9 2.6 %copy-start.3 = (bf16[1024,2048]{0,1:T(8,128)(2,1)}, bf16[1024,2048]{0,1:T(8,128)(2,1)S(1)}, u32[]{:S(2)}) copy-start(bf16[1024,2048]{0,1:T(8,128)(2,1)S(1)} %get-tuple-element.12) | copy-start | bytes 12582916
  24.9 3.2 %copy-start.5 = (bf16[1024,2048]{0,1:T(8,128)(2,1)}, bf16[1024,2048]{0,1:T(8,128)(2,1)S(1)}, u32[]{:S(2)}) copy-start(bf16[1024,2048]{0,1:T(8,128)(2,1)S(1)} %get-tuple-element.11) | copy-start | bytes 12582916
  24.9 4.5 %copy-start.1 = (bf16[1024,2048]{0,1:T(8,128)(2,1)}, bf16[1024,2048]{0,1:T(8,128)(2,1)S(1)}, u32[]{:S(2)}) copy-start(bf16[1024,2048]{0,1:T(8,128)(2,1)S(1)} %get-tuple-element.9) | copy-start | bytes 12582916
  24.9 5.8 %copy-start.9 = (bf16[1024,2048]{0,1:T(8,128)(2,1)}, bf16[1024,2048]{0,1:T(8,128)(2,1)S(1)}, u32[]{:S(2)}) copy-start(bf16[1024,2048]{0,1:T(8,128)(2,1)S(1)} %get-tuple-element.10) | copy-start | bytes 12582916
  29.4 2.9 %copy-start.7 = (bf16[1024,2048]{1,0:T(8,128)(2,1)S(1)}, bf16[1024,2048]{1,0:T(8,128)(2,1)}, u32[]{:S(2)}) copy-start(bf16[1024,2048]{1,0:T(8,128)(2,1)} %param.8) | copy-start | bytes 12582916
  30.7 3.9 %copy-start.14 = (bf16[1024,2048]{0,1:T(8,128)(2,1)S(1)}, bf16[1024,2048]{0,1:T(8,128)(2,1)}, u32[]{:S(2)}) copy-start(bf16[1024,2048]{0,1:T(8,128)(2,1)} %get-tuple-element.13) | copy-start | bytes 12582916
  31.0 8.4 %collective-permute-start.4 = (bf16[4,128,2048]{1,2,0:T(8,128)(2,1)S(1)}, bf16[4,128,2048]{1,2,0:T(8,128)(2,1)S(1)}, u32[]{:S(2)}, u32[]{:S(2)}) collective-permute-start(bf16[4,128,2048]{1,2,0:T(8,128)(2,1)S(1)} %pad_maximum_fusion), channel_id=1, source_target_pairs={{0,2},{2,0},{4,6},{6,4},{8,10},{10,8},{12,14},{14,12},{16,18},{18,... | collective-permute-start | bytes 6291464 | tf_op jit(solution)/shard_map/ppermute | solution.py:14
  33.9 18.8 %collective-permute-start = (bf16[128,2048]{1,0:T(8,128)(2,1)}, bf16[128,2048]{1,0:T(8,128)(2,1)S(1)}, u32[]{:S(2)}, u32[]{:S(2)}) collective-permute-start(bf16[128,2048]{1,0:T(8,128)(2,1)} %convolution_convert_fusion), channel_id=1, source_target_pairs={{0,2},{2,0},{4,6},{6,4},{8,10},{10,8},{12,14},{14,12},{16,18},{18,... | collective-permute-start | bytes 1572872 | tf_op jit(solution)/shard_map/ppermute | solution.py:14
  39.6 3.4 %copy-start.11 = (f32[4,128,2048]{1,2,0:T(8,128)}, f32[4,128,2048]{1,2,0:T(8,128)S(1)}, u32[]{:S(2)}) copy-start(f32[4,128,2048]{1,2,0:T(8,128)S(1)} %convert_element_type.108) | copy-start | bytes 12582916
  43.1 47.8 %collective-permute-start.5 = (bf16[3,128,2048]{1,2,0:T(8,128)(2,1)}, bf16[3,128,2048]{1,2,0:T(8,128)(2,1)}, u32[]{:S(2)}, u32[]{:S(2)}) collective-permute-start(bf16[3,128,2048]{1,2,0:T(8,128)(2,1)} %get-tuple-element.7), channel_id=1, source_target_pairs={{0,4},{4,0},{2,6},{6,2},{8,12},{12,8},{10,14},{14,10},{16,20},{20,... | collective-permute-start | bytes 4718600 | tf_op jit(solution)/shard_map/ppermute | solution.py:14
  53.8 36.6 %collective-permute-start.1 = (bf16[128,2048]{1,0:T(8,128)(2,1)S(1)}, bf16[128,2048]{1,0:T(8,128)(2,1)S(1)}, u32[]{:S(2)}, u32[]{:S(2)}) collective-permute-start(bf16[128,2048]{1,0:T(8,128)(2,1)S(1)} %add_convert_fusion.2), channel_id=1, source_target_pairs={{0,4},{4,0},{2,6},{6,2},{8,12},{12,8},{10,14},{14,10},{16,20},{20,... | collective-permute-start | bytes 1572872 | tf_op jit(solution)/shard_map/ppermute | solution.py:14
  55.9 36.6 %copy-start.12 = (f32[3,128,2048]{1,2,0:T(8,128)S(1)}, f32[3,128,2048]{1,2,0:T(8,128)}, u32[]{:S(2)}) copy-start(f32[3,128,2048]{1,2,0:T(8,128)} %get-tuple-element.8) | copy-start | bytes 9437188
  90.6 12.7 %collective-permute-start.2 = (bf16[128,2048]{1,0:T(8,128)(2,1)S(1)}, bf16[128,2048]{1,0:T(8,128)(2,1)S(1)}, u32[]{:S(2)}, u32[]{:S(2)}) collective-permute-start(bf16[128,2048]{1,0:T(8,128)(2,1)S(1)} %add_convert_fusion.1), channel_id=1, source_target_pairs={{0,8},{8,0},{2,10},{10,2},{4,12},{12,4},{6,14},{14,6},{16,24},{24,... | collective-permute-start | bytes 1572872 | tf_op jit(solution)/shard_map/ppermute | solution.py:14
  92.5 2.2 %copy-start.10 = (bf16[1024,2048]{0,1:T(8,128)(2,1)S(1)}, bf16[1024,2048]{0,1:T(8,128)(2,1)}, u32[]{:S(2)}) copy-start(bf16[1024,2048]{0,1:T(8,128)(2,1)} %copy-done.9) | copy-start | bytes 12582916
  92.8 13.0 %copy-start.6 = (bf16[1024,2048]{0,1:T(8,128)(2,1)S(1)}, bf16[1024,2048]{0,1:T(8,128)(2,1)}, u32[]{:S(2)}) copy-start(bf16[1024,2048]{0,1:T(8,128)(2,1)} %copy-done.5) | copy-start | bytes 12582916
  92.8 42.2 %collective-permute-start.6 = (bf16[2,128,2048]{1,2,0:T(8,128)(2,1)S(1)}, bf16[2,128,2048]{1,2,0:T(8,128)(2,1)S(1)}, u32[]{:S(2)}, u32[]{:S(2)}) collective-permute-start(bf16[2,128,2048]{1,2,0:T(8,128)(2,1)S(1)} %get-tuple-element.5), channel_id=1, source_target_pairs={{0,8},{8,0},{2,10},{10,2},{4,12},{12,4},{6,14},{14,6},{16,24},{24,... | collective-permute-start | bytes 3145736 | tf_op jit(solution)/shard_map/ppermute | solution.py:14
  103.4 36.2 %collective-permute-start.3 = (bf16[128,2048]{1,0:T(8,128)(2,1)S(1)}, bf16[128,2048]{1,0:T(8,128)(2,1)S(1)}, u32[]{:S(2)}, u32[]{:S(2)}) collective-permute-start(bf16[128,2048]{1,0:T(8,128)(2,1)S(1)} %add_convert_fusion), channel_id=1, source_target_pairs={{0,16},{16,0},{2,18},{18,2},{4,20},{20,4},{6,22},{22,6},{8,24},{24... | collective-permute-start | bytes 1572872 | tf_op jit(solution)/shard_map/ppermute | solution.py:14
  107.1 32.6 %copy-start.4 = (bf16[1024,2048]{0,1:T(8,128)(2,1)S(1)}, bf16[1024,2048]{0,1:T(8,128)(2,1)}, u32[]{:S(2)}) copy-start(bf16[1024,2048]{0,1:T(8,128)(2,1)} %copy-done.3) | copy-start | bytes 12582916
  135.1 5.8 %copy-start.2 = (bf16[1024,2048]{0,1:T(8,128)(2,1)S(1)}, bf16[1024,2048]{0,1:T(8,128)(2,1)}, u32[]{:S(2)}) copy-start(bf16[1024,2048]{0,1:T(8,128)(2,1)} %copy-done.1) | copy-start | bytes 12582916
  135.3 26.2 %collective-permute-start.7 = (bf16[1,128,2048]{1,2,0:T(8,128)(2,1)S(1)}, bf16[1,128,2048]{1,2,0:T(8,128)(2,1)S(1)}, u32[]{:S(2)}, u32[]{:S(2)}) collective-permute-start(bf16[1,128,2048]{1,2,0:T(8,128)(2,1)S(1)} %fusion.17), channel_id=1, source_target_pairs={{0,16},{16,0},{2,18},{18,2},{4,20},{20,4},{6,22},{22,6},{8,24},{24... | collective-permute-start | bytes 1572872 | tf_op jit(solution)/shard_map/ppermute | solution.py:14
  141.0 22.1 %copy-start.8 = (bf16[1024,2048]{1,0:T(8,128)(2,1)S(1)}, bf16[1024,2048]{1,0:T(8,128)(2,1)}, u32[]{:S(2)}) copy-start(bf16[1024,2048]{1,0:T(8,128)(2,1)} %param.8) | copy-start | bytes 12582916
Sparse Core Ops, SparseCore 0:
  165.2 29.2 all-reduce.2
where the time goes:
time: 208 us; the launch traced here: 205 us
  waiting for transfers between devices  110 us (53%)
  matrix products  36.7 us (18%)
  other arithmetic  19.6 us (9%)
  between operations  14.3 us (7%)
  local copies, waits for them, and re-layouts  12.3 us (6%)
  starting transfers between devices  11.3 us (5%)
    ppermute x8, waiting for transfers between devices, swapped(): return lax.ppermute(block, axis, route)  87.6 us
    psum x1, waiting for transfers between devices, per_device(): lax.psum(query_grad.astype(jnp.bfloat16), 'head').astype(jnp.float32)  22.8 us
    dot_general x7, matrix products, contract_rows(): lax.dot_general(left, right, (((0,), (0,)), ((), ())), preferred_element_...  16.7 us
    dot_general x6, matrix products, contract_cols(): lax.dot_general(left, right, (((1,), (1,)), ((), ())), preferred_element_...  12.7 us
    unnamed x33, local copies, waits for them, and re-layouts  12.3 us
    ppermute x8, starting transfers between devices, swapped(): return lax.ppermute(block, axis, route)  11.3 us
    convert_element_type x1, other arithmetic, scale_by(): (shaped * weights[:, height, :, None]).reshape(rows_here, columns)  8.66 us
    dot_general x1, matrix products, per_device(): jnp.dot(key_rows, state_low, preferred_element_type=jnp.float32)  6.65 us
  transfers between devices with their start and end apart: 9, of which 5 were waited for; matrix products, arithmetic and copies ran while one was open for 18% of the time, Pallas kernels for 0%

commit v1 on v0

v1 whole, which is shorter than its diff:
```python
import functools

import jax
import jax.numpy as jnp
from jax import lax
from jax.experimental import pallas as pl
from jax.experimental.pallas import tpu as pltpu
from jax.sharding import PartitionSpec as P

F32 = jnp.float32
BF16 = jnp.bfloat16
PARTS = 4
TILE = 256


def dot(left, right, dims=((1,), (0,))):
    return lax.dot_general(left, right, (dims, ((), ())), preferred_element_type=F32)


def exchange(block, mask):
    count = lax.axis_size("seq")
    return lax.ppermute(block, "seq", [(i, i ^ mask) for i in range(count)])


def head_sum(partial):
    count = lax.axis_size("head")
    stride = 1
    while stride < count:
        other = lax.ppermute(partial, "head", [(i, i ^ stride) for i in range(count)])
        partial = (partial.astype(F32) + other.astype(F32)).astype(BF16)
        stride *= 2
    return partial


def level_weights(index_ref, table_ref, level):
    table = table_ref[level]
    picks = table.shape[0]
    row = index_ref[level : level + 1, :]
    ids = lax.broadcasted_iota(jnp.int32, (picks, row.shape[1]), 0)
    hot = (jnp.broadcast_to(row, ids.shape) == ids).astype(F32)
    hot = jnp.concatenate([hot, hot], axis=0).astype(BF16)
    high = table.astype(BF16).astype(F32)
    terms = jnp.concatenate([high, table - high], axis=0).astype(BF16)
    return dot(terms, hot, ((0,), (0,)))


def scaled_rows(grad, weight_row, head_size, heads):
    parts = []
    for h in range(heads):
        part = grad[h * head_size : (h + 1) * head_size, :]
        weight = jnp.broadcast_to(weight_row(h), part.shape)
        parts.append((weight * part.astype(F32)).astype(BF16))
    return jnp.concatenate(parts, axis=0)


def slot_kernel(levels, head_size, make_transpose, pos_ref, *refs):
    refs = list(refs)
    q_ref, k_ref, v_ref, g_ref, index_ref, table_ref = refs[:6]
    del refs[:6]
    outs = [(refs.pop(0), refs.pop(0)) for _ in levels]
    if make_transpose:
        gt_ref = refs.pop(0)
    q_t, k_t, weights = refs
    step = pl.program_id(0)
    pos = pos_ref[0]

    @pl.when(step == 0)
    def _():
        q_t[...] = q_ref[...].T
        k_t[...] = k_ref[...].T
        for i, level in enumerate(levels):
            weights[i] = level_weights(index_ref, table_ref, level)

    if make_transpose:
        gt_ref[...] = g_ref[...].T
    else:
        gt_ref = g_ref
    width = v_ref.shape[1]
    heads = width // head_size
    first = (place_of(step) ^ (pos & 3)) * heads
    for i, (level, (send, keep)) in enumerate(zip(levels, outs)):
        bit = (pos >> (level - 1)) & 1

        def put(value):
            @pl.when(step < PARTS // 2)
            def _():
                send[0] = value

            @pl.when(step >= PARTS // 2)
            def _():
                keep[0] = value

        @pl.when(bit == 1)
        def _():
            scaled = scaled_rows(
                gt_ref[...], lambda h: weights[i, pl.ds(first + h, 1), :], head_size, heads
            )
            put(dot(q_t[...], scaled, ((1,), (1,))).astype(BF16))

        @pl.when(bit == 0)
        def _():
            put(dot(k_t[...], v_ref[...]).astype(BF16))


def place_of(step):
    half = PARTS // 2
    return jnp.where(step < half, 2 * step + 1, 2 * (step - half))


def slots(pos, q, k, v, g, index, table, levels, head_size, make_transpose):
    tokens, state = q.shape
    columns = v.shape[1]
    width = columns // PARTS
    depth, picks, heads = table.shape

    def quarter(s, p):
        return place_of(s) ^ (p[0] & 3)

    whole = lambda s, p: (0, 0)
    half = PARTS // 2
    slab = jax.ShapeDtypeStruct((half, state, width), BF16)
    out_shape = [slab] * (2 * len(levels))
    out_specs = [
        pl.BlockSpec((1, state, width), lambda s, p: (jnp.minimum(s, half - 1), 0, 0)),
        pl.BlockSpec((1, state, width), lambda s, p: (jnp.maximum(s - half, 0), 0, 0)),
    ] * len(levels)
    if make_transpose:
        g_spec = pl.BlockSpec((tokens, width), lambda s, p: (0, quarter(s, p)))
        out_shape.append(jax.ShapeDtypeStruct((columns, tokens), BF16))
        out_specs.append(pl.BlockSpec((width, tokens), lambda s, p: (quarter(s, p), 0)))
    else:
        g_spec = pl.BlockSpec((width, tokens), lambda s, p: (quarter(s, p), 0))
    return pl.pallas_call(
        functools.partial(slot_kernel, levels, head_size, make_transpose),
        grid_spec=pltpu.PrefetchScalarGridSpec(
            num_scalar_prefetch=1,
            grid=(PARTS,),
            in_specs=[
                pl.BlockSpec((tokens, state), whole),
                pl.BlockSpec((tokens, state), whole),
                pl.BlockSpec((tokens, width), lambda s, p: (0, quarter(s, p))),
                g_spec,
                pl.BlockSpec(index.shape, whole),
                pl.BlockSpec(table.shape, lambda s, p: (0, 0, 0)),
            ],
            out_specs=out_specs,
            scratch_shapes=[
                pltpu.VMEM((state, tokens), BF16),
                pltpu.VMEM((state, tokens), BF16),
                pltpu.VMEM((len(levels), heads, tokens), F32),
            ],
        ),
        out_shape=out_shape,
        cost_estimate=pl.CostEstimate(
            flops=2 * tokens * state * columns * len(levels) * 2,
            bytes_accessed=4 * tokens * columns + 4 * tokens * columns,
            transcendentals=0,
        ),
        name="slots_" + "_".join(map(str, levels)),
    )(pos, q, k, v, g, index, table)


def local_kernel(head_size, q_ref, k_ref, v_ref, gt_ref, index_ref, table_ref, qg_ref, kg_ref):
    step = pl.program_id(0)
    heads = table_ref.shape[2]
    weights = level_weights(index_ref, table_ref, 0)
    scaled = scaled_rows(gt_ref[...], lambda h: weights[h : h + 1, :], head_size, heads)
    tile = gt_ref.shape[1]
    for j in range(v_ref.shape[0] // tile):

        @pl.when(step == j)
        def _():
            rows = (j + 1) * tile
            grads = dot(v_ref[:rows, :], scaled)
            s_ids = lax.broadcasted_iota(jnp.int32, grads.shape, 0)
            t_ids = lax.broadcasted_iota(jnp.int32, grads.shape, 1) + j * tile
            grads = jnp.where(s_ids <= t_ids, grads, 0.0).astype(BF16)
            qg_ref[...] = dot(k_ref[:rows, :], grads, ((0,), (0,)))
            part = dot(grads, q_ref[...])
            if j:
                kg_ref[: rows - tile, :] += part[: rows - tile]
            kg_ref[rows - tile : rows, :] = part[rows - tile :]


def local_terms(q, k, v, gt, index, table, head_size):
    tokens, state = q.shape
    columns = v.shape[1]
    tile = min(TILE, tokens)
    whole = lambda j: (0, 0)
    return pl.pallas_call(
        functools.partial(local_kernel, head_size),
        grid=(tokens // tile,),
        in_specs=[
            pl.BlockSpec((tile, state), lambda j: (j, 0)),
            pl.BlockSpec((tokens, state), whole),
            pl.BlockSpec((tokens, columns), whole),
            pl.BlockSpec((columns, tile), lambda j: (0, j)),
            pl.BlockSpec((index.shape[0], tile), lambda j: (0, j)),
            pl.BlockSpec(table.shape, lambda j: (0, 0, 0)),
        ],
        out_specs=[
            pl.BlockSpec((state, tile), lambda j: (0, j)),
            pl.BlockSpec((tokens, state), whole),
        ],
        out_shape=[
            jax.ShapeDtypeStruct((state, tokens), F32),
            jax.ShapeDtypeStruct((tokens, state), F32),
        ],
        cost_estimate=pl.CostEstimate(
            flops=2 * tokens * tokens * columns,
            bytes_accessed=4 * tokens * columns,
            transcendentals=0,
        ),
        name="local_terms",
    )(q, k, v, gt, index, table)


def query_kernel(levels, pieces, head_size, last, pos_ref, *refs):
    refs = list(refs)
    gt_ref, index_ref, table_ref, base_ref = refs[:4]
    del refs[:4]
    arrived = refs[: -3]
    out_ref, weights, total = refs[-3:]
    step = pl.program_id(0)
    pos = pos_ref[0]
    width = gt_ref.shape[0]
    heads = width // head_size

    @pl.when(step == 0)
    def _():
        for i, level in enumerate(levels):
            weights[i] = level_weights(index_ref, table_ref, level)
        total[...] = base_ref[...]

    first = (step ^ (pos & 3)) * heads
    for i, level in enumerate(levels):
        bit = (pos >> (level - 1)) & 1

        @pl.when(bit == 1)
        def _():
            scaled = scaled_rows(
                gt_ref[...], lambda h: weights[i, pl.ds(first + h, 1), :], head_size, heads
            )
            for r in range(PARTS):

                @pl.when(step == r)
                def _():
                    total[...] += dot(pieces(arrived, level, r), scaled)

    @pl.when(step == PARTS - 1)
    def _():
        if last:
            out_ref[...] = total[...].T.astype(BF16)
        else:
            out_ref[...] = total[...]


def query_terms(pos, gt, index, table, base, arrived, levels, pieces, head_size, last):
    state, tokens = base.shape
    columns = gt.shape[0]
    width = columns // PARTS
    whole = lambda s, p: (0, 0)
    shape = (tokens, state) if last else (state, tokens)
    return pl.pallas_call(
        functools.partial(query_kernel, levels, pieces, head_size, last),
        grid_spec=pltpu.PrefetchScalarGridSpec(
            num_scalar_prefetch=1,
            grid=(PARTS,),
            in_specs=[
                pl.BlockSpec((width, tokens), lambda s, p: (s ^ (p[0] & 3), 0)),
                pl.BlockSpec(index.shape, whole),
                pl.BlockSpec(table.shape, lambda s, p: (0, 0, 0)),
                pl.BlockSpec(base.shape, whole),
            ]
            + [whole_spec(a, 2) for a in arrived],
            out_specs=pl.BlockSpec(shape, whole),
            scratch_shapes=[
                pltpu.VMEM((len(levels), table.shape[2], tokens), F32),
                pltpu.VMEM((state, tokens), F32),
            ],
        ),
        out_shape=jax.ShapeDtypeStruct(shape, BF16 if last else F32),
        cost_estimate=pl.CostEstimate(
            flops=4 * tokens * state * columns * len(levels),
            bytes_accessed=2 * tokens * columns,
            transcendentals=0,
        ),
        name="query_terms_" + "_".join(map(str, levels)),
    )(pos, gt, index, table, base, *arrived)


def whole_spec(array, n_args):
    zeros = (0,) * array.ndim
    if n_args == 2:
        return pl.BlockSpec(array.shape, lambda s, p: zeros)
    return pl.BlockSpec(array.shape, lambda s: zeros)


def gather_state(levels, pieces, arrived, pos, state_ref):
    for r in range(PARTS):
        total = jnp.zeros(state_ref.shape[1:], F32)
        for level in levels:
            clear = ((pos >> (level - 1)) & 1) == 0
            piece = pieces(arrived, level, r).astype(F32)
            total = total + jnp.where(clear, piece, 0.0)
        state_ref[r] = total.astype(BF16)


def key_kernel(levels, pieces, pos_ref, v_ref, base_ref, *refs):
    arrived, (out_ref, state, total) = refs[:-3], refs[-3:]
    step = pl.program_id(0)

    @pl.when(step == 0)
    def _():
        gather_state(levels, pieces, arrived, pos_ref[0], state)
        total[...] = base_ref[...]

    total[...] += dot(v_ref[...], state[step], ((1,), (1,)))

    @pl.when(step == PARTS - 1)
    def _():
        out_ref[...] = total[...].astype(BF16)


def key_terms(pos, v, base, arrived, levels, pieces):
    tokens, state = base.shape
    columns = v.shape[1]
    width = columns // PARTS
    whole = lambda s, p: (0, 0)
    return pl.pallas_call(
        functools.partial(key_kernel, levels, pieces),
        grid_spec=pltpu.PrefetchScalarGridSpec(
            num_scalar_prefetch=1,
            grid=(PARTS,),
            in_specs=[
                pl.BlockSpec((tokens, width), lambda s, p: (0, s ^ (p[0] & 3))),
                pl.BlockSpec(base.shape, whole),
            ]
            + [whole_spec(a, 2) for a in arrived],
            out_specs=pl.BlockSpec(base.shape, whole),
            scratch_shapes=[
                pltpu.VMEM((PARTS, state, width), BF16),
                pltpu.VMEM(base.shape, F32),
            ],
        ),
        out_shape=jax.ShapeDtypeStruct(base.shape, BF16),
        cost_estimate=pl.CostEstimate(
            flops=4 * tokens * state * columns,
            bytes_accessed=2 * tokens * columns,
            transcendentals=0,
        ),
        name="key_terms",
    )(pos, v, base, *arrived)


def value_kernel(levels, pieces, head_size, pos_ref, q_ref, k_ref, gt_ref, index_ref, table_ref, *refs):
    arrived, (out_ref, state, masked, weights) = refs[:-4], refs[-4:]
    step = pl.program_id(0)
    pos = pos_ref[0]
    tokens = q_ref.shape[0]
    tile = min(TILE, tokens)
    heads = gt_ref.shape[0] // head_size

    @pl.when(step == 0)
    def _():
        gather_state(levels, pieces, arrived, pos, state)
        weights[...] = level_weights(index_ref, table_ref, 0)
        for i in range(tokens // tile):
            low = i * tile
            scores = dot(k_ref[low : low + tile, :], q_ref[low:, :], ((1,), (1,)))
            s_ids = lax.broadcasted_iota(jnp.int32, scores.shape, 0)
            t_ids = lax.broadcasted_iota(jnp.int32, scores.shape, 1)
            masked[low : low + tile, low:] = jnp.where(s_ids <= t_ids, scores, 0.0).astype(BF16)

    first = (step ^ (pos & 3)) * heads
    scaled = scaled_rows(
        gt_ref[...], lambda h: weights[pl.ds(first + h, 1), :], head_size, heads
    )
    for i in range(tokens // tile):
        low = i * tile
        near = dot(masked[low : low + tile, low:], scaled[:, low:], ((1,), (1,)))
        far = dot(k_ref[low : low + tile, :], state[step])
        out_ref[low : low + tile, :] = (near + far).astype(BF16)


def value_terms(pos, q, k, gt, index, table, arrived, levels, pieces, head_size):
    tokens, state = q.shape
    columns = gt.shape[0]
    width = columns // PARTS
    whole = lambda s, p: (0, 0)
    return pl.pallas_call(
        functools.partial(value_kernel, levels, pieces, head_size),
        grid_spec=pltpu.PrefetchScalarGridSpec(
            num_scalar_prefetch=1,
            grid=(PARTS,),
            in_specs=[
                pl.BlockSpec(q.shape, whole),
                pl.BlockSpec(k.shape, whole),
                pl.BlockSpec((width, tokens), lambda s, p: (s ^ (p[0] & 3), 0)),
                pl.BlockSpec(index.shape, whole),
                pl.BlockSpec(table.shape, lambda s, p: (0, 0, 0)),
            ]
            + [whole_spec(a, 2) for a in arrived],
            out_specs=pl.BlockSpec((tokens, width), lambda s, p: (0, s ^ (p[0] & 3))),
            scratch_shapes=[
                pltpu.VMEM((PARTS, state, width), BF16),
                pltpu.VMEM((tokens, tokens), BF16),
                pltpu.VMEM((table.shape[2], tokens), F32),
            ],
        ),
        out_shape=jax.ShapeDtypeStruct((tokens, columns), BF16),
        cost_estimate=pl.CostEstimate(
            flops=2 * tokens * tokens * columns,
            bytes_accessed=4 * tokens * columns,
            transcendentals=0,
        ),
        name="value_terms",
    )(pos, q, k, gt, index, table, *arrived)


def add(left, right):
    return (left.astype(F32) + right.astype(F32)).astype(BF16)


def low_piece(arrived, level, r):
    one, two_here, two_core = arrived
    if level == 1:
        place = r ^ 1
        return one[1 - place % 2, place >> 1]
    if r % 2 == 0:
        return two_here[(r ^ 2) >> 1]
    return two_core[(r ^ 3) >> 1]


def high_piece(arrived, level, r):
    here, chip, core = arrived
    i = level - 3
    if r == 0:
        return here[i]
    if r == 2:
        return chip[i]
    return core[r >> 1, i]


def any_piece(arrived, level, r):
    if level < 3:
        return low_piece(arrived[:3], level, r)
    return high_piece(arrived[3:], level, r)


def per_device(queries, key_rows, value_rows, out_grad, level_index, level_table):
    columns = value_rows.shape[1]
    head_size = columns // level_table.shape[2]
    depth = lax.axis_size("seq").bit_length() - 1
    pos = lax.axis_index("seq").astype(jnp.int32)[None]
    index = level_index.T
    table = level_table
    low, high = (1, 2), tuple(range(3, depth + 1))

    *halves, gt = slots(
        pos, queries, key_rows, value_rows, out_grad, index, table, high, head_size, True
    )
    send = jnp.stack(halves[0::2], axis=1)
    keep = jnp.stack(halves[1::2], axis=1)
    got = exchange(send, 1)
    leave = add(keep[1], got[1])
    own = add(keep[0], got[0])
    send1, keep1, send2, keep2 = slots(
        pos, queries, key_rows, value_rows, gt, index, table, low, head_size, False
    )
    own = add(own, exchange(leave, 2))
    one = exchange(jnp.stack([send1, keep1]), 1)
    half2 = add(keep2, exchange(send2, 1))
    two_here = exchange(half2, 2)
    two_core = exchange(two_here, 1)
    query_local, key_local = local_terms(
        queries, key_rows, value_rows, gt, index, table, head_size
    )
    here = []
    for j in range(2, depth):
        got = exchange(own, (1 << (j + 1)) - 4)
        here.append(got[0])
        own = add(own[1:], got[1:])
    here = jnp.stack(here)
    low_arrived = (one, two_here, two_core)
    query_low = query_terms(
        pos, gt, index, table, query_local, low_arrived, low, low_piece, head_size, False
    )
    chip = exchange(here, 2)
    core = exchange(jnp.stack([here, chip]), 1)
    high_arrived = (here, chip, core)
    arrived = low_arrived + high_arrived
    key_part = key_terms(pos, value_rows, key_local, arrived, low + high, any_piece)
    query_part = query_terms(
        pos, gt, index, table, query_low, high_arrived, high, high_piece, head_size, True
    )
    key_grad = head_sum(key_part)
    query_grad = head_sum(query_part)
    value_grad = value_terms(
        pos, queries, key_rows, gt, index, table, arrived, low + high, any_piece, head_size
    )
    return query_grad, key_grad, value_grad


def solution(mesh):
    return jax.shard_map(
        per_device,
        mesh=mesh,
        in_specs=(
            P("seq", None),
            P("seq", None),
            P("seq", "head"),
            P("seq", "head"),
            P("seq", None),
            P(None, None, "head"),
        ),
        out_specs=(P("seq", None), P("seq", None), P("seq", "head")),
        check_vma=False,
    )
```

time: 208 us -> 93.9 us (0.45); the launches traced: 205 us -> 93.3 us
  waiting for transfers between devices: 110 us -> 18.7 us
  Pallas kernels: 0 us -> 55.1 us
  matrix products: 36.7 us -> 0 us
  between operations: 14.3 us -> 0.78 us
  other arithmetic: 19.6 us -> 6.96 us
  local copies, waits for them, and re-layouts: 12.3 us -> 1.66 us
    ppermute x8 -> x12, waiting for transfers between devices: 87.6 us -> 18.7 us  [the longest x10 18.7 us: exchange(): return lax.ppermute(block, 'seq', [(i, i ^ mask) for i in range(count)])]
    pallas_call x0 -> x7, Pallas kernels: none -> 55.1 us  [the longest x2 16.5 us: slots(): pl.pallas_call(functools.partial(slot_kernel, levels, head_size, make_tra...]
    dot_general x15 -> x0, matrix products: 36.7 us -> none  [the longest x7 16.7 us: contract_rows(): lax.dot_general(left, right, (((0,), (0,)), ((), ())), preferred_element_...]
    psum x1 -> x0, waiting for transfers between devices: 22.8 us -> none  [per_device(): lax.psum(query_grad.astype(jnp.bfloat16), 'head').astype(jnp.float32)]
    unnamed x33 -> x16, local copies, waits for them, and re-layouts: 12.3 us -> 1.65 us
    convert_element_type x10 -> x6, other arithmetic: 15.3 us -> 4.7 us  [the longest x4 3.15 us: add(): return (left.astype(F32) + right.astype(F32)).astype(BF16)]
    ppermute x8 -> x12, starting transfers between devices: 11.3 us -> 10.2 us  [the longest x10 8.75 us: exchange(): return lax.ppermute(block, 'seq', [(i, i ^ mask) for i in range(count)])]
  transfers between devices with their start and end apart: 9 -> 12, of which waited for: 5 -> 5; matrix products, arithmetic and copies ran while one was open for 18% -> 3% of each run, Pallas kernels for 0% -> 43%
where the time goes in v1:
time: 93.9 us; the launch traced here: 93.3 us
  Pallas kernels  55.1 us (59%)
  waiting for transfers between devices  18.7 us (20%)
  starting transfers between devices  10.2 us (11%)
  other arithmetic  6.96 us (7%)
  local copies, waits for them, and re-layouts  1.66 us (2%)
    ppermute x10, waiting for transfers between devices, exchange(): return lax.ppermute(block, 'seq', [(i, i ^ mask) for i in range(count)])  18.7 us
    pallas_call x2, Pallas kernels, slots(): pl.pallas_call(functools.partial(slot_kernel, levels, head_size, make_tra...  16.5 us
    pallas_call x2, Pallas kernels, query_terms(): pl.pallas_call(functools.partial(query_kernel, levels, pieces, head_size,...  13.2 us
    pallas_call x1, Pallas kernels, local_terms(): pl.pallas_call(functools.partial(local_kernel, head_size), grid=(tokens /...  10.5 us
    pallas_call x1, Pallas kernels, value_terms(): pl.pallas_call(functools.partial(value_kernel, levels, pieces, head_size)...  9.13 us
    ppermute x10, starting transfers between devices, exchange(): return lax.ppermute(block, 'seq', [(i, i ^ mask) for i in range(count)])  8.75 us
    pallas_call x1, Pallas kernels, key_terms(): pl.pallas_call(functools.partial(key_kernel, levels, pieces), grid_spec=p...  5.78 us
    convert_element_type x4, other arithmetic, add(): return (left.astype(F32) + right.astype(F32)).astype(BF16)  3.15 us
  transfers between devices with their start and end apart: 12, of which 5 were waited for; matrix products, arithmetic and copies ran while one was open for 3% of the time, Pallas kernels for 43%

profile of v1, /device:TPU:15, one launch (start us, length us, event | category | flops | bytes accessed | tf_op | source)
XLA Modules:
  0.0 93.3 jit_solution(8135589352859244467)
XLA Ops:
  0.6 8.9 %slots_3_4.1 = (bf16[2,128,512]{2,1,0:T(8,128)(2,1)}, bf16[2,128,512]{2,1,0:T(8,128)(2,1)}, bf16[2,128,512]{2,1,0:T(8,128)(2,1)}, bf16[2,128,512]{2,1,0:T(8,128)(2,1)}, bf16[2048,1024]{1,0:T(8,128)(2,1)}) custom-call(s32[1]{0:T(128)} %bitcast.pos_ref, bf16[1024,128]{1,0:T(8,128)(2,1)} %q_ref.3, bf16[1024,128]{1,0:T(8,128)(2,1)} %k_ref.3, ...), custom_call_target="tpu_custom_call" | custom-call | flops 2147483648 | bytes 16777216 | tf_op jit(solution)/shard_map/slots_3_4/pallas_call | solution.py:133
  9.5 1.1 %pad_maximum_fusion.1 = bf16[2,2,128,512]{3,2,1,0:T(8,128)(2,1)S(1)} fusion(bf16[2,1,128,512]{3,2,1,0:T(8,128)(2,1)} %bitcast.26, bf16[2,1,128,512]{3,2,1,0:T(8,128)(2,1)} %bitcast.25), kind=kLoop, calls=%fused_computation.3 | loop fusion | flops 262144 | bytes 1048576 | tf_op jit(solution)/shard_map/stack | solution.py:463
  10.6 0.8 collective-permute-start.4
  11.4 1.5 %collective-permute-done.4 = bf16[2,2,128,512]{3,2,1,0:T(8,128)(2,1)S(1)} collective-permute-done((bf16[2,2,128,512]{3,2,1,0:T(8,128)(2,1)S(1)}, bf16[2,2,128,512]{3,2,1,0:T(8,128)(2,1)S(1)}, u32[]{:S(2)}, u32[]{:S(2)}) %collective-permute-start.4) | collective-permute-done | bytes 524320 | tf_op jit(solution)/shard_map/ppermute | solution.py:22
  12.9 1.0 %fusion.2 = bf16[2,128,512]{2,1,0:T(8,128)(2,1)S(1)} fusion(bf16[2,2,128,512]{3,2,1,0:T(8,128)(2,1)S(1)} %collective-permute-done.4, bf16[2,1,128,512]{3,2,1,0:T(8,128)(2,1)} %bitcast.21, bf16[2,1,128,512]{3,2,1,0:T(8,128)(2,1)} %bitcast.19), kind=kLoop, calls=%fused_computation.13 | loop fusion | flops 655360 | bytes 1048576 | tf_op jit(solution)/shard_map/convert_element_type | solution.py:422
  13.9 0.3 collective-permute-start.5
  14.2 7.3 %collective-permute-done.5 = bf16[2,128,512]{2,1,0:T(8,128)(2,1)S(1)} collective-permute-done((bf16[2,128,512]{2,1,0:T(8,128)(2,1)S(1)}, bf16[2,128,512]{2,1,0:T(8,128)(2,1)S(1)}, u32[]{:S(2)}, u32[]{:S(2)}) %collective-permute-start.5) | collective-permute-done | bytes 262176 | tf_op jit(solution)/shard_map/ppermute | solution.py:22
  21.5 1.1 %fusion = bf16[2,128,512]{2,1,0:T(8,128)(2,1)S(1)} fusion(bf16[2,128,512]{2,1,0:T(8,128)(2,1)S(1)} %collective-permute-done.5, bf16[2,1,128,512]{3,2,1,0:T(8,128)(2,1)} %bitcast.20, bf16[2,1,128,512]{3,2,1,0:T(8,128)(2,1)} %bitcast.22, bf16[2,2,128,512]{3,2,1,0:T(8,128)(2,1)S(1)} %collective-permute-done.4), kind=kLoop, calls=%fused_computation.6 | loop fusion | flops 1179648 | bytes 1310720 | tf_op jit(solution)/shard_map/convert_element_type | solution.py:422
  22.6 0.1 collective-permute-start.6
  22.6 7.6 %slots_1_2.1 = (bf16[2,128,512]{2,1,0:T(8,128)(2,1)}, bf16[2,128,512]{2,1,0:T(8,128)(2,1)}, bf16[2,128,512]{2,1,0:T(8,128)(2,1)}, bf16[2,128,512]{2,1,0:T(8,128)(2,1)}) custom-call(s32[1]{0:T(128)} %bitcast.pos_ref, bf16[1024,128]{1,0:T(8,128)(2,1)} %q_ref.3, bf16[1024,128]{1,0:T(8,128)(2,1)} %k_ref.3, bf16[1024,2048]{1,0:T(8,128)(2,1)} %v_ref.3, ...), custom_call_target="tpu_custom_call" | custom-call | flops 2147483648 | bytes 16777216 | tf_op jit(solution)/shard_map/slots_1_2/pallas_call | solution.py:133
  30.2 0.7 collective-permute-start.1
  31.0 0.0 collective-permute-done.6
  31.0 3.4 %collective-permute-start.7 = (bf16[1,128,512]{2,1,0:T(8,128)(2,1)S(1)}, bf16[1,128,512]{2,1,0:T(8,128)(2,1)S(1)}, u32[]{:S(2)}, u32[]{:S(2)}) collective-permute-start(bf16[1,128,512]{2,1,0:T(8,128)(2,1)S(1)} %add_convert_fusion.5), channel_id=1, source_target_pairs={{0,24},{2,26},{4,28},{6,30},{8,16},{10,18},{12,20},{14,22},{16,8},... | collective-permute-start | bytes 393224 | tf_op jit(solution)/shard_map/ppermute | solution.py:22
  34.4 0.0 collective-permute-done.1
  34.4 1.0 %add_convert_fusion.4 = bf16[2,128,512]{2,1,0:T(8,128)(2,1)S(1)} fusion(bf16[2,128,512]{2,1,0:T(8,128)(2,1)S(1)} %collective-permute-done.1, bf16[2,128,512]{2,1,0:T(8,128)(2,1)} %get-tuple-element.18), kind=kLoop, calls=%fused_computation.11 | loop fusion | flops 524288 | bytes 786432 | tf_op jit(solution)/shard_map/convert_element_type | solution.py:422
  35.4 0.1 collective-permute-start.2
  35.5 5.5 %collective-permute-done.7 = bf16[1,128,512]{2,1,0:T(8,128)(2,1)S(1)} collective-permute-done((bf16[1,128,512]{2,1,0:T(8,128)(2,1)S(1)}, bf16[1,128,512]{2,1,0:T(8,128)(2,1)S(1)}, u32[]{:S(2)}, u32[]{:S(2)}) %collective-permute-start.7) | collective-permute-done | bytes 131104 | tf_op jit(solution)/shard_map/ppermute | solution.py:22
  41.1 0.0 copy-start
  41.1 0.1 collective-permute-start.8
  41.2 1.1 %pad_maximum_fusion = bf16[2,2,128,512]{3,2,1,0:T(8,128)(2,1)S(1)} fusion(bf16[1,2,128,512]{3,2,1,0:T(8,128)(2,1)} %bitcast.24, bf16[1,2,128,512]{3,2,1,0:T(8,128)(2,1)} %bitcast.23), kind=kLoop, calls=%fused_computation | loop fusion | flops 262144 | bytes 1048576 | tf_op jit(solution)/shard_map/stack | solution.py:472
  42.3 0.7 collective-permute-start
  43.0 0.1 collective-permute-done.2.refs_5_.refs_1_
  43.1 0.0 copy-start.5
  43.1 1.2 %collective-permute-start.3 = (bf16[2,128,512]{2,1,0:T(8,128)(2,1)S(1)}, bf16[2,128,512]{2,1,0:T(8,128)(2,1)S(1)}, u32[]{:S(2)}, u32[]{:S(2)}) collective-permute-start(bf16[2,128,512]{2,1,0:T(8,128)(2,1)S(1)} %collective-permute-done.2.refs_5_.refs_1_), channel_id=1, source_target_pairs={{0,2},{2,0},{4,6},{6,4},{8,10},{10,8},{12,14},{14,12},{16,18},{18,... | collective-permute-start | bytes 786440 | tf_op jit(solution)/shard_map/ppermute | solution.py:22
  44.2 4.2 %collective-permute-done.8.refs_5_.refs_4_ = bf16[2,128,512]{2,1,0:T(8,128)(2,1)S(1)} collective-permute-done((bf16[2,128,512]{2,1,0:T(8,128)(2,1)S(1)}, bf16[2,128,512]{2,1,0:T(8,128)(2,1)S(1)}, u32[]{:S(2)}, u32[]{:S(2)}) %collective-permute-start.8) | collective-permute-done | bytes 262176 | tf_op jit(solution)/shard_map/ppermute | solution.py:22
  48.4 0.0 copy-start.2
  48.5 0.1 pad_maximum_fusion.2
  48.5 1.5 %collective-permute-start.9 = (bf16[2,2,128,512]{3,2,1,0:T(8,128)(2,1)S(1)}, bf16[2,2,128,512]{3,2,1,0:T(8,128)(2,1)S(1)}, u32[]{:S(2)}, u32[]{:S(2)}) collective-permute-start(bf16[2,2,128,512]{3,2,1,0:T(8,128)(2,1)S(1)} %pad_maximum_fusion.2), channel_id=1, source_target_pairs={{0,2},{2,0},{4,6},{6,4},{8,10},{10,8},{12,14},{14,12},{16,18},{18,... | collective-permute-start | bytes 1572872 | tf_op jit(solution)/shard_map/ppermute | solution.py:22
  50.0 10.5 %local_terms.1 = (f32[128,1024]{1,0:T(8,128)}, f32[1024,128]{1,0:T(8,128)}) custom-call(bf16[1024,128]{1,0:T(8,128)(2,1)} %q_ref.3, bf16[1024,128]{1,0:T(8,128)(2,1)} %k_ref.3, bf16[1024,2048]{1,0:T(8,128)(2,1)} %v_ref.3, bf16[2048,1024]{1,0:T(8,128)(2,1)} %get-tuple-element.14.gt_ref.refs_3_.refs_0_, s32[5,1024]{1,0:T(8,128)} %bitcast.29, f32[5,8,32]{2,1,0:T(8,128)} %table_ref.3), custom_call_target="tpu_custom_call" | custom-call | flops 4294967296 | bytes 8388608 | tf_op jit(solution)/shard_map/local_terms/pallas_call | solution.py:190
  60.5 0.0 copy-done
  60.5 0.0 copy-done.5
  60.5 0.0 copy-done.2
  60.5 0.0 collective-permute-done.refs_4_.refs_0_
  60.6 0.0 copy-start.3
  60.6 0.0 collective-permute-done.3.refs_6_.refs_2_
  60.6 0.0 copy-start.6
  60.6 0.8 copy-done.3
  61.4 0.1 copy-done.6
  61.4 7.4 %query_terms_1_2.1.refs_3_ = f32[128,1024]{1,0:T(8,128)} custom-call(s32[1]{0:T(128)} %bitcast.pos_ref, bf16[2048,1024]{1,0:T(8,128)(2,1)} %get-tuple-element.14.gt_ref.refs_3_.refs_0_, s32[5,1024]{1,0:T(8,128)} %bitcast.30, f32[5,8,32]{2,1,0:T(8,128)} %table_ref.3, f32[128,1024]{1,0:T(8,128)} %get-tuple-element.15.refs_3_, ...), custom_call_target="tpu_custom_call" | custom-call | flops 2147483648 | bytes 4194304 | tf_op jit(solution)/shard_map/query_terms_1_2/pallas_call | solution.py:264
  68.8 0.0 collective-permute-done.9.refs_6_.refs_5_
  68.8 0.0 copy-start.4
  68.8 0.8 copy-done.4
  69.6 5.8 %key_terms.1 = bf16[1024,128]{1,0:T(8,128)(2,1)} custom-call(s32[1]{0:T(128)} %bitcast.pos_ref, bf16[1024,2048]{1,0:T(8,128)(2,1)} %v_ref.3, f32[1024,128]{1,0:T(8,128)} %get-tuple-element.24.base_ref, bf16[2,2,128,512]{3,2,1,0:T(8,128)(2,1)} %copy-done.3, bf16[2,128,512]{2,1,0:T(8,128)(2,1)} %copy-done.5, bf16[2,128,512]{2,1,0:T(8,128)(2,1)} %copy-done.6, ...), custom_call_target="tpu_custom_call" | custom-call | flops 1073741824 | bytes 4194304 | tf_op jit(solution)/shard_map/key_terms/pallas_call | solution.py:330
  75.4 0.2 collective-permute-start.11
  75.6 5.8 %query_terms_3_4.1 = bf16[1024,128]{1,0:T(8,128)(2,1)} custom-call(s32[1]{0:T(128)} %bitcast.pos_ref, bf16[2048,1024]{1,0:T(8,128)(2,1)} %get-tuple-element.14.gt_ref.refs_3_.refs_0_, s32[5,1024]{1,0:T(8,128)} %bitcast.31, f32[5,8,32]{2,1,0:T(8,128)} %table_ref.3, f32[128,1024]{1,0:T(8,128)} %query_terms_1_2.1.refs_3_, bf16[2,128,512]{2,1,0:T(8,128)(2,1)} %copy-done, ...), custom_call_target="tpu_custom_call" | custom-call | flops 2147483648 | bytes 4194304 | tf_op jit(solution)/shard_map/query_terms_3_4/pallas_call | solution.py:264
  81.4 0.0 copy-start.1
  81.4 0.0 copy-start.7
  81.4 1.2 %collective-permute-start.10 = (bf16[1024,128]{1,0:T(8,128)(2,1)}, bf16[1024,128]{1,0:T(8,128)(2,1)S(1)}, u32[]{:S(2)}, u32[]{:S(2)}) collective-permute-start(bf16[1024,128]{1,0:T(8,128)(2,1)} %query_terms_3_4.1), channel_id=1, source_target_pairs={{0,1},{1,0},{2,3},{3,2},{4,5},{5,4},{6,7},{7,6},{8,9},{9,8},{10,11... | collective-permute-start | bytes 786440 | tf_op jit(solution)/shard_map/ppermute | solution.py:29
  82.6 9.1 %value_terms.1 = bf16[1024,2048]{1,0:T(8,128)(2,1)} custom-call(s32[1]{0:T(128)} %bitcast.pos_ref, bf16[1024,128]{1,0:T(8,128)(2,1)} %q_ref.3, bf16[1024,128]{1,0:T(8,128)(2,1)} %k_ref.3, bf16[2048,1024]{1,0:T(8,128)(2,1)} %get-tuple-element.14.gt_ref.refs_3_.refs_0_, s32[5,1024]{1,0:T(8,128)} %bitcast.32, f32[5,8,32]{2,1,0:T(8,128)} %table_ref.3, ...), custom_call_target="tpu_custom_call" | custom-call | flops 4294967296 | bytes 8388608 | tf_op jit(solution)/shard_map/value_terms/pallas_call | solution.py:391
  91.8 0.0 collective-permute-done.11
  91.8 0.0 copy-done.1
  91.8 0.8 add_convert_fusion
  92.6 0.0 collective-permute-done.10
  92.6 0.0 copy-done.7
  92.6 0.8 add_convert_fusion.1
  (3 shorter events, 0.1 us)
Async XLA Ops:
  10.6 2.3 %collective-permute-start.4 = (bf16[2,2,128,512]{3,2,1,0:T(8,128)(2,1)S(1)}, bf16[2,2,128,512]{3,2,1,0:T(8,128)(2,1)S(1)}, u32[]{:S(2)}, u32[]{:S(2)}) collective-permute-start(bf16[2,2,128,512]{3,2,1,0:T(8,128)(2,1)S(1)} %pad_maximum_fusion.1), channel_id=1, source_target_pairs={{0,2},{2,0},{4,6},{6,4},{8,10},{10,8},{12,14},{14,12},{16,18},{18,... | collective-permute-start | bytes 1572872 | tf_op jit(solution)/shard_map/ppermute | solution.py:22
  13.9 7.6 %collective-permute-start.5 = (bf16[2,128,512]{2,1,0:T(8,128)(2,1)S(1)}, bf16[2,128,512]{2,1,0:T(8,128)(2,1)S(1)}, u32[]{:S(2)}, u32[]{:S(2)}) collective-permute-start(bf16[2,128,512]{2,1,0:T(8,128)(2,1)S(1)} %fusion.2), channel_id=1, source_target_pairs={{0,4},{2,6},{4,0},{6,2},{8,12},{10,14},{12,8},{14,10},{16,20},{18,... | collective-permute-start | bytes 786440 | tf_op jit(solution)/shard_map/ppermute | solution.py:22
  22.6 8.4 %collective-permute-start.6 = (bf16[2,128,512]{2,1,0:T(8,128)(2,1)S(1)}, bf16[2,128,512]{2,1,0:T(8,128)(2,1)S(1)}, u32[]{:S(2)}, u32[]{:S(2)}) collective-permute-start(bf16[2,128,512]{2,1,0:T(8,128)(2,1)S(1)} %fusion), channel_id=1, source_target_pairs={{0,8},{2,10},{4,12},{6,14},{8,0},{10,2},{12,4},{14,6},{16,24},{18,... | collective-permute-start | bytes 786440 | tf_op jit(solution)/shard_map/ppermute | solution.py:22
  30.2 4.2 %collective-permute-start.1 = (bf16[2,128,512]{2,1,0:T(8,128)(2,1)}, bf16[2,128,512]{2,1,0:T(8,128)(2,1)S(1)}, u32[]{:S(2)}, u32[]{:S(2)}) collective-permute-start(bf16[2,128,512]{2,1,0:T(8,128)(2,1)} %get-tuple-element.19), channel_id=1, source_target_pairs={{0,2},{2,0},{4,6},{6,4},{8,10},{10,8},{12,14},{14,12},{16,18},{18,... | collective-permute-start | bytes 786440 | tf_op jit(solution)/shard_map/ppermute | solution.py:22
  31.0 10.0 %collective-permute-start.7 = (bf16[1,128,512]{2,1,0:T(8,128)(2,1)S(1)}, bf16[1,128,512]{2,1,0:T(8,128)(2,1)S(1)}, u32[]{:S(2)}, u32[]{:S(2)}) collective-permute-start(bf16[1,128,512]{2,1,0:T(8,128)(2,1)S(1)} %add_convert_fusion.5), channel_id=1, source_target_pairs={{0,24},{2,26},{4,28},{6,30},{8,16},{10,18},{12,20},{14,22},{16,8},... | collective-permute-start | bytes 393224 | tf_op jit(solution)/shard_map/ppermute | solution.py:22
  35.4 7.6 %collective-permute-start.2 = (bf16[2,128,512]{2,1,0:T(8,128)(2,1)S(1)}, bf16[2,128,512]{2,1,0:T(8,128)(2,1)S(1)}, u32[]{:S(2)}, u32[]{:S(2)}) collective-permute-start(bf16[2,128,512]{2,1,0:T(8,128)(2,1)S(1)} %add_convert_fusion.4), channel_id=1, source_target_pairs={{0,4},{2,6},{4,0},{6,2},{8,12},{10,14},{12,8},{14,10},{16,20},{18,... | collective-permute-start | bytes 786440 | tf_op jit(solution)/shard_map/ppermute | solution.py:22
  41.1 19.4 %copy-start = (bf16[2,128,512]{2,1,0:T(8,128)(2,1)}, bf16[2,128,512]{2,1,0:T(8,128)(2,1)S(1)}, u32[]{:S(2)}) copy-start(bf16[2,128,512]{2,1,0:T(8,128)(2,1)S(1)} %get-tuple-element.26.refs_4_.refs_3_) | copy-start | bytes 786436
  41.1 7.3 %collective-permute-start.8 = (bf16[2,128,512]{2,1,0:T(8,128)(2,1)S(1)}, bf16[2,128,512]{2,1,0:T(8,128)(2,1)S(1)}, u32[]{:S(2)}, u32[]{:S(2)}) collective-permute-start(bf16[2,128,512]{2,1,0:T(8,128)(2,1)S(1)} %get-tuple-element.26.refs_4_.refs_3_), channel_id=1, source_target_pairs={{0,4},{2,6},{4,0},{6,2},{8,12},{10,14},{12,8},{14,10},{16,20},{18,... | collective-permute-start | bytes 786440 | tf_op jit(solution)/shard_map/ppermute | solution.py:22
  42.3 18.2 %collective-permute-start = (bf16[2,2,128,512]{3,2,1,0:T(8,128)(2,1)S(1)}, bf16[2,2,128,512]{3,2,1,0:T(8,128)(2,1)S(1)}, u32[]{:S(2)}, u32[]{:S(2)}) collective-permute-start(bf16[2,2,128,512]{3,2,1,0:T(8,128)(2,1)S(1)} %pad_maximum_fusion), channel_id=1, source_target_pairs={{0,2},{2,0},{4,6},{6,4},{8,10},{10,8},{12,14},{14,12},{16,18},{18,... | collective-permute-start | bytes 1572872 | tf_op jit(solution)/shard_map/ppermute | solution.py:22
  43.1 17.5 %copy-start.5 = (bf16[2,128,512]{2,1,0:T(8,128)(2,1)}, bf16[2,128,512]{2,1,0:T(8,128)(2,1)S(1)}, u32[]{:S(2)}) copy-start(bf16[2,128,512]{2,1,0:T(8,128)(2,1)S(1)} %collective-permute-done.2.refs_5_.refs_1_) | copy-start | bytes 786436
  43.1 17.5 %collective-permute-start.3 = (bf16[2,128,512]{2,1,0:T(8,128)(2,1)S(1)}, bf16[2,128,512]{2,1,0:T(8,128)(2,1)S(1)}, u32[]{:S(2)}, u32[]{:S(2)}) collective-permute-start(bf16[2,128,512]{2,1,0:T(8,128)(2,1)S(1)} %collective-permute-done.2.refs_5_.refs_1_), channel_id=1, source_target_pairs={{0,2},{2,0},{4,6},{6,4},{8,10},{10,8},{12,14},{14,12},{16,18},{18,... | collective-permute-start | bytes 786440 | tf_op jit(solution)/shard_map/ppermute | solution.py:22
  48.4 12.1 %copy-start.2 = (bf16[2,128,512]{2,1,0:T(8,128)(2,1)}, bf16[2,128,512]{2,1,0:T(8,128)(2,1)S(1)}, u32[]{:S(2)}) copy-start(bf16[2,128,512]{2,1,0:T(8,128)(2,1)S(1)} %collective-permute-done.8.refs_5_.refs_4_) | copy-start | bytes 786436
  48.5 20.3 %collective-permute-start.9 = (bf16[2,2,128,512]{3,2,1,0:T(8,128)(2,1)S(1)}, bf16[2,2,128,512]{3,2,1,0:T(8,128)(2,1)S(1)}, u32[]{:S(2)}, u32[]{:S(2)}) collective-permute-start(bf16[2,2,128,512]{3,2,1,0:T(8,128)(2,1)S(1)} %pad_maximum_fusion.2), channel_id=1, source_target_pairs={{0,2},{2,0},{4,6},{6,4},{8,10},{10,8},{12,14},{14,12},{16,18},{18,... | collective-permute-start | bytes 1572872 | tf_op jit(solution)/shard_map/ppermute | solution.py:22
  60.6 0.8 copy-start.3
  60.6 0.9 copy-start.6
  68.8 0.8 copy-start.4
  75.4 16.4 %collective-permute-start.11 = (bf16[1024,128]{1,0:T(8,128)(2,1)}, bf16[1024,128]{1,0:T(8,128)(2,1)S(1)}, u32[]{:S(2)}, u32[]{:S(2)}) collective-permute-start(bf16[1024,128]{1,0:T(8,128)(2,1)} %key_terms.1), channel_id=1, source_target_pairs={{0,1},{1,0},{2,3},{3,2},{4,5},{5,4},{6,7},{7,6},{8,9},{9,8},{10,11... | collective-permute-start | bytes 786440 | tf_op jit(solution)/shard_map/ppermute | solution.py:29
  81.4 10.4 %copy-start.1 = (bf16[1024,128]{1,0:T(8,128)(2,1)S(1)}, bf16[1024,128]{1,0:T(8,128)(2,1)}, u32[]{:S(2)}) copy-start(bf16[1024,128]{1,0:T(8,128)(2,1)} %key_terms.1) | copy-start | bytes 786436
  81.4 11.2 %copy-start.7 = (bf16[1024,128]{1,0:T(8,128)(2,1)S(1)}, bf16[1024,128]{1,0:T(8,128)(2,1)}, u32[]{:S(2)}) copy-start(bf16[1024,128]{1,0:T(8,128)(2,1)} %query_terms_3_4.1) | copy-start | bytes 786436
  81.4 11.2 %collective-permute-start.10 = (bf16[1024,128]{1,0:T(8,128)(2,1)}, bf16[1024,128]{1,0:T(8,128)(2,1)S(1)}, u32[]{:S(2)}, u32[]{:S(2)}) collective-permute-start(bf16[1024,128]{1,0:T(8,128)(2,1)} %query_terms_3_4.1), channel_id=1, source_target_pairs={{0,1},{1,0},{2,3},{3,2},{4,5},{5,4},{6,7},{7,6},{8,9},{9,8},{10,11... | collective-permute-start | bytes 786440 | tf_op jit(solution)/shard_map/ppermute | solution.py:29
